TPU v7x, 32 devices: a whole 2x2x4 slice. The times are simulated.
32 devices in a mesh: dp: 4 (over y, x), tensor: 8 (over z, core).
Axes of the slice: x: 2, y: 2, z: 4, core: 2. Of those that a mesh axis runs over, the one named last changes fastest.
Arguments:
- tokens: bfloat16 [2048, 8192], P('dp', 'tensor'), may hold values from -6 to 6
- cotangent: bfloat16 [2048, 8192], P('dp', 'tensor'), may hold values from -6 to 6
- w_first: bfloat16 [32, 256, 1024], P('tensor'), may hold values from -0.375 to 0.375
- w_second: bfloat16 [128, 256, 256], P('tensor'), may hold values from -0.375 to 0.375
- third_weight_blocks: bfloat16 [128, 256, 256], P('tensor'), may hold values from -0.375 to 0.375
- w_fourth: bfloat16 [32, 1024, 256], P('tensor'), may hold values from -0.1875 to 0.1875
Outputs:
- layer_out: bfloat16 [2048, 8192], P('dp', 'tensor')
- tokens_grad: bfloat16 [2048, 8192], P('dp', 'tensor')
- grad_first: float32 [32, 256, 1024], P('tensor')
- grad_second: float32 [128, 256, 256], P('tensor')
- grad_third: float32 [128, 256, 256], P('tensor')
- grad_fourth: float32 [32, 1024, 256], P('tensor')
All inputs are finite; a program needn't handle non-finite values.
Results may differ from a plain program's by a relative error of at most 0.0095.
Values may be sent and summed in bfloat16 or wider, within the bound.
No kernel may reach another device: no remote copies, remote signals or barrier semaphores. Data moves between devices by JAX's collectives and lax.ppermute only.
A program may use at most 128 MiB of HBM per device.

v0:
```python
import math
import jax
import jax.numpy as jnp
from jax import lax
from jax.sharding import PartitionSpec as P


def gelu_parts(value_in):
    cdf_part = 0.5 * (1.0 + lax.erf(value_in * 0.7071067811865476))
    slope_part = cdf_part + value_in * jnp.exp(-0.5 * value_in * value_in) * 0.3989422804014327
    return (value_in * cdf_part, slope_part)


def body(tokens, cotangent, w_first, w_second, third_weight_blocks, w_fourth):
    row_count = tokens.shape[0]
    width_dev = w_first.shape[0]
    block_width = w_first.shape[1]
    hidden_dev = w_second.shape[0]
    groups = lax.axis_size("tensor")
    in_blocks = width_dev * groups
    hid_blocks = hidden_dev * groups
    sub_width = block_width // in_blocks
    grad_scale = 1.0 / math.sqrt(row_count * lax.axis_size("dp"))
    inputs_view = tokens.reshape(row_count, width_dev, block_width)
    cot_view = cotangent.reshape(row_count, width_dev, block_width)
    first_factor_parts = w_first.reshape(width_dev, block_width, groups, hidden_dev, sub_width)
    first_view = w_first.reshape(width_dev, block_width, hid_blocks, sub_width)
    second_view = w_second.reshape(hidden_dev, in_blocks, sub_width, block_width)
    second_split = w_second.reshape(hidden_dev, groups, width_dev, sub_width, block_width)
    third_split = third_weight_blocks.reshape(hidden_dev, block_width, groups, width_dev, sub_width)
    fourth_view = w_fourth.reshape(width_dev, hid_blocks, sub_width, block_width)
    fourth_split = w_fourth.reshape(width_dev, groups, hidden_dev, sub_width, block_width)
    first_out = jnp.einsum(
        "tai,aigbc->gabct", inputs_view, first_factor_parts, preferred_element_type=jnp.float32
    )
    first_out = first_out.astype(jnp.bfloat16)
    received = lax.all_to_all(first_out, "tensor", split_axis=0, concat_axis=0, tiled=True)
    count = received.shape[4]
    flat_rows = received.reshape(in_blocks * hidden_dev, sub_width, count)
    spread = flat_rows
    count = flat_rows.shape[2]
    spread_view = flat_rows.reshape(in_blocks, hidden_dev, sub_width, count)
    pre_act = jnp.einsum(
        "abct,bacj->bjt", spread_view, second_view, preferred_element_type=jnp.float32
    )
    gelu_val, gelu_slope = gelu_parts(pre_act)
    activated = gelu_val.astype(jnp.bfloat16)
    third_factor_output = jnp.einsum(
        "bjt,bjgac->gbact", activated, third_split, preferred_element_type=jnp.float32
    )
    third_factor_output = third_factor_output.astype(jnp.bfloat16)
    received = lax.all_to_all(
        third_factor_output, "tensor", split_axis=0, concat_axis=0, tiled=True
    )
    count = received.shape[4]
    flat_rows = received.reshape(hid_blocks * width_dev, sub_width, count)
    merged = received.reshape(hid_blocks, width_dev, sub_width, count)
    out_part = jnp.einsum("bact,abck->akt", merged, fourth_view, preferred_element_type=jnp.float32)
    out_rows = out_part.astype(jnp.bfloat16)
    layer_out = jnp.transpose(out_rows, (2, 0, 1)).reshape(row_count, width_dev * block_width)
    third_grad = jnp.einsum(
        "tak,agbck->gbact", cot_view, fourth_split, preferred_element_type=jnp.float32
    )
    third_grad = third_grad.astype(jnp.bfloat16)
    collected_view = flat_rows.reshape(hid_blocks, width_dev, sub_width, row_count)
    grad_fourth = jnp.einsum(
        "bact,tak->abck", collected_view, cot_view, preferred_element_type=jnp.float32
    )
    grad_fourth = (grad_fourth * grad_scale).reshape(width_dev, hid_blocks * sub_width, block_width)
    returned = lax.all_to_all(third_grad, "tensor", split_axis=0, concat_axis=0, tiled=True)
    activation_gradient = jnp.einsum(
        "gbact,bjgac->bjt", returned, third_split, preferred_element_type=jnp.float32
    )
    pre_grad = (activation_gradient * gelu_slope).astype(jnp.bfloat16)
    grad_third = jnp.einsum(
        "bjt,gbact->bjgac", activated, returned, preferred_element_type=jnp.float32
    )
    grad_third = (grad_third * grad_scale).reshape(hidden_dev, block_width, block_width)
    first_grad = jnp.einsum(
        "bjt,bgacj->gbact", pre_grad, second_split, preferred_element_type=jnp.float32
    )
    first_grad = first_grad.astype(jnp.bfloat16)
    spread_view = spread.reshape(in_blocks, hidden_dev, sub_width, row_count)
    grad_second = jnp.einsum(
        "abct,bjt->bacj", spread_view, pre_grad, preferred_element_type=jnp.float32
    )
    grad_second = (grad_second * grad_scale).reshape(hidden_dev, block_width, block_width)
    back_first = lax.all_to_all(first_grad, "tensor", split_axis=0, concat_axis=0, tiled=True)
    back_view = back_first.reshape(hid_blocks, width_dev, sub_width, row_count)
    tokens_grad = jnp.einsum(
        "bact,aibc->tai", back_view, first_view, preferred_element_type=jnp.float32
    )
    tokens_grad = tokens_grad.astype(jnp.bfloat16).reshape(row_count, width_dev * block_width)
    grad_first = jnp.einsum(
        "tai,bact->aibc", inputs_view, back_view, preferred_element_type=jnp.float32
    )
    grad_first = (grad_first * grad_scale).reshape(width_dev, block_width, hid_blocks * sub_width)
    grad_first, grad_second, grad_third, grad_fourth = (
        lax.psum(grad_first.astype(jnp.bfloat16), "dp").astype(jnp.float32),
        lax.psum(grad_second.astype(jnp.bfloat16), "dp").astype(jnp.float32),
        lax.psum(grad_third.astype(jnp.bfloat16), "dp").astype(jnp.float32),
        lax.psum(grad_fourth.astype(jnp.bfloat16), "dp").astype(jnp.float32),
    )
    return (layer_out, tokens_grad, grad_first, grad_second, grad_third, grad_fourth)


def solution(mesh):
    return jax.shard_map(
        body,
        mesh=mesh,
        in_specs=(
            P("dp", "tensor"),
            P("dp", "tensor"),
            P("tensor", None, None),
            P("tensor", None, None),
            P("tensor", None, None),
            P("tensor", None, None),
        ),
        out_specs=(
            P("dp", "tensor"),
            P("dp", "tensor"),
            P("tensor", None, None),
            P("tensor", None, None),
            P("tensor", None, None),
            P("tensor", None, None),
        ),
        check_vma=False,
    )
```

profile of v0, /device:TPU:0, one launch (start us, length us, event | category | flops | bytes accessed | tf_op | source)
XLA Modules:
  0.0 628.3 jit_solution(12406556423778622042)
XLA Ops:
  7.2 0.0 copy-start
  7.2 2.0 reshape.60
  9.2 4.0 copy.64
  13.2 2.9 convert_bitcast_fusion.3
  16.1 2.5 copy.66
  18.5 6.3 %all-to-all-start = ((bf16[8,4,16,8,512]{4,3,2,1,0:T(8,128)(2,1)}), bf16[8,4,16,8,512]{4,3,2,1,0:T(8,128)(2,1)}, u32[]{:S(2)}, u32[]{:S(2)}) async-start(bf16[8,4,16,8,512]{4,3,2,1,0:T(8,128)(2,1)} %copy.66), calls=%async_computation | async-start | bytes 8388608 | tf_op jit(solution)/shard_map/all_to_all | solution.py:37
  24.9 2.6 reshape.67
  27.5 3.1 convert_bitcast_fusion.1
  30.6 2.5 copy.73
  33.1 85.9 %all-to-all-done = bf16[8,4,16,8,512]{4,3,2,1,0:T(8,128)(2,1)} async-done(((bf16[8,4,16,8,512]{4,3,2,1,0:T(8,128)(2,1)}), bf16[8,4,16,8,512]{4,3,2,1,0:T(8,128)(2,1)}, u32[]{:S(2)}, u32[]{:S(2)}) %all-to-all-start) | async-done | bytes 4194336 | tf_op jit(solution)/shard_map/all_to_all | solution.py:37
  119.0 4.6 all-to-all-start.2
  123.6 3.9 copy.68
  127.5 0.0 copy-done
  127.5 7.4 %fusion.9 = (bf16[16,256,512]{1,2,0:T(8,128)(2,1)}, f32[16,512,256,1]{2,1,0,3:T(8,128)}) fusion(bf16[32,16,8,512]{3,2,1,0:T(8,128)(2,1)} %bitcast.3, bf16[16,256,256]{2,1,0:T(8,128)(2,1)S(1)} %copy-done), kind=kOutput, calls=%fused_computation.12 | convolution fusion | flops 1084227584 | bytes 18874368 | tf_op jit(solution)/shard_map/abct,bacj->bjt/dot_general | solution.py:43
  134.9 82.7 %all-to-all-done.2 = bf16[8,16,4,8,512]{4,3,1,2,0:T(8,128)(2,1)} async-done(((bf16[8,16,4,8,512]{4,3,1,2,0:T(8,128)(2,1)}), bf16[8,16,4,8,512]{4,3,1,2,0:T(8,128)(2,1)}, u32[]{:S(2)}, u32[]{:S(2)}) %all-to-all-start.2) | async-done | bytes 4194336 | tf_op jit(solution)/shard_map/all_to_all | solution.py:70
  217.6 7.9 %fusion.5 = bf16[16,256,512]{1,2,0:T(8,128)(2,1)S(1)} fusion(f32[16,512,256,1]{2,1,0,3:T(8,128)} %get-tuple-element.29, bf16[8,16,4,8,512]{4,3,1,2,0:T(8,128)(2,1)} %all-to-all-done.2, bf16[16,256,8,4,8]{1,4,3,2,0:T(8,128)(2,1)} %bitcast.118), kind=kOutput, calls=%fused_computation.6 | convolution fusion | flops 1094713344 | bytes 18874368 | tf_op jit(solution)/shard_map/gbact,bjgac->bjt/dot_general | solution.py:71
  225.4 0.0 copy-start.5
  225.5 1.3 convert_bitcast_fusion
  226.8 0.7 copy-done.5
  227.5 2.5 copy.77
  230.0 0.0 copy-start.2
  230.0 4.9 all-to-all-start.3
  234.9 0.0 copy-done.2
  234.9 3.5 fusion.57
  238.4 0.7 convert_bitcast_fusion.2
  239.0 2.4 copy.70
  241.4 87.3 %all-to-all-done.3 = bf16[8,16,4,8,512]{4,3,2,1,0:T(8,128)(2,1)} async-done(((bf16[8,16,4,8,512]{4,3,2,1,0:T(8,128)(2,1)}), bf16[8,16,4,8,512]{4,3,2,1,0:T(8,128)(2,1)}, u32[]{:S(2)}, u32[]{:S(2)}) %all-to-all-start.3) | async-done | bytes 4194336 | tf_op jit(solution)/shard_map/all_to_all | solution.py:88
  328.7 4.5 all-to-all-start.1
  333.2 0.0 all-reduce.3.cloned.1.call-start
  333.3 4.7 multiply_convert_fusion.1
  338.0 2.5 copy.87
  340.5 6.0 fusion.33
  346.5 7.0 %fusion.32 = bf16[4,256,128,8]{1,2,3,0:T(8,128)(2,1)S(1)} fusion(bf16[128,4,8,512]{3,2,1,0:T(8,128)(2,1)} %bitcast.26, bf16[512,4,256,1]{2,1,0,3:T(4,128)(2,1)S(1)} %bitcast.114), kind=kOutput, calls=%fused_computation.35 | convolution fusion | flops 1075838976 | bytes 7340032 | tf_op jit(solution)/shard_map/tai,bact->aibc/dot_general | solution.py:94
  353.5 0.0 copy-start.4
  353.5 2.5 copy.162
  356.0 71.2 %all-to-all-done.1 = bf16[8,16,4,8,512]{4,3,2,1,0:T(8,128)(2,1)} async-done(((bf16[8,16,4,8,512]{4,3,2,1,0:T(8,128)(2,1)}), bf16[8,16,4,8,512]{4,3,2,1,0:T(8,128)(2,1)}, u32[]{:S(2)}, u32[]{:S(2)}) %all-to-all-start.1) | async-done | bytes 4194336 | tf_op jit(solution)/shard_map/all_to_all | solution.py:52
  427.2 0.0 copy-done.4
  427.2 7.2 %multiply_convert_fusion = bf16[4,128,8,256]{3,1,2,0:T(8,128)(2,1)S(1)} fusion(bf16[128,4,8,512]{3,2,1,0:T(8,128)(2,1)} %bitcast.12, bf16[512,4,256,1]{2,1,0,3:T(4,128)(2,1)S(1)} %bitcast.116), kind=kOutput, calls=%fused_computation.27 | convolution fusion | flops 1075838976 | bytes 7340032 | tf_op jit(solution)/shard_map/bact,tak->abck/dot_general | solution.py:66
  434.4 2.5 copy.161
  436.9 0.0 copy-start.3
  436.9 0.0 all-reduce.3.cloned.1.call-update
  437.0 1.6 copy-done.3
  438.5 3.5 bitcast_convert_fusion
  442.0 1.3 copy.92
  443.3 4.2 bitcast_convert_fusion.1
  447.5 1.3 copy.91
  448.8 160.9 %all-reduce.3.cloned.1.call-done = (bf16[4,256,1024]{1,2,0:T(8,128)(2,1)}, bf16[16,256,256]{2,1,0:T(8,128)(2,1)}, bf16[16,256,256]{2,1,0:T(8,128)(2,1)}, bf16[4,1024,256]{2,1,0:T(8,128)(2,1)}) async-done(((bf16[4,256,1024]{1,2,0:T(8,128)(2,1)}, bf16[16,256,256]{2,1,0:T(8,128)(2,1)}, bf16[16,256,256]{2,1,0:T(8,128)(2,1)}, bf16[4,1024,256]{2,1,0:T(8,128)(2,1)}), (bf16[4,256,1024]{1,2,0:T(8,128)(2,1)}, ...) | async-done | bytes 8388624 | tf_op jit(solution)/shard_map/psum | solution.py:99
  609.7 0.0 copy-start.8
  609.7 4.3 copy.93
  614.0 0.0 copy-start.7
  614.0 0.0 copy-done.8
  614.0 2.5 convert_element_type.102
  616.4 0.0 copy-start.6
  616.4 0.0 copy-done.7
  616.4 0.0 copy-start.1
  616.4 2.6 convert_element_type.105
  619.0 0.0 copy-done.6
  619.0 2.4 convert_element_type.108
  621.4 0.0 copy-done.1
Async XLA Ops:
  7.2 120.3 %copy-start = (bf16[16,256,256]{2,1,0:T(8,128)(2,1)S(1)}, bf16[16,256,256]{2,1,0:T(8,128)(2,1)}, u32[]{:S(2)}) copy-start(bf16[16,256,256]{2,1,0:T(8,128)(2,1)} %param.9) | copy-start | bytes 6291460
  18.5 100.4 %all-to-all-start = ((bf16[8,4,16,8,512]{4,3,2,1,0:T(8,128)(2,1)}), bf16[8,4,16,8,512]{4,3,2,1,0:T(8,128)(2,1)}, u32[]{:S(2)}, u32[]{:S(2)}) async-start(bf16[8,4,16,8,512]{4,3,2,1,0:T(8,128)(2,1)} %copy.66), calls=%async_computation | async-start | bytes 8388608 | tf_op jit(solution)/shard_map/all_to_all | solution.py:37
  119.0 98.6 %all-to-all-start.2 = ((bf16[8,16,4,8,512]{4,3,1,2,0:T(8,128)(2,1)}), bf16[8,16,4,8,512]{4,3,1,2,0:T(8,128)(2,1)}, u32[]{:S(2)}, u32[]{:S(2)}) async-start(bf16[8,16,4,8,512]{4,3,1,2,0:T(8,128)(2,1)} %copy.73), calls=%async_computation.2 | async-start | bytes 8388608 | tf_op jit(solution)/shard_map/all_to_all | solution.py:70
  225.4 2.0 copy-start.5
  230.0 4.9 copy-start.2
  230.0 98.7 %all-to-all-start.3 = ((bf16[8,16,4,8,512]{4,3,2,1,0:T(8,128)(2,1)}), bf16[8,16,4,8,512]{4,3,2,1,0:T(8,128)(2,1)}, u32[]{:S(2)}, u32[]{:S(2)}) async-start(bf16[8,16,4,8,512]{4,3,2,1,0:T(8,128)(2,1)} %copy.77), calls=%async_computation.3 | async-start | bytes 8388608 | tf_op jit(solution)/shard_map/all_to_all | solution.py:88
  328.7 98.6 %all-to-all-start.1 = ((bf16[8,16,4,8,512]{4,3,2,1,0:T(8,128)(2,1)}), bf16[8,16,4,8,512]{4,3,2,1,0:T(8,128)(2,1)}, u32[]{:S(2)}, u32[]{:S(2)}) async-start(bf16[8,16,4,8,512]{4,3,2,1,0:T(8,128)(2,1)} %copy.70), calls=%async_computation.1 | async-start | bytes 8388608 | tf_op jit(solution)/shard_map/all_to_all | solution.py:52
  333.2 276.5 %all-reduce.3.cloned.1.call-start = ((), (), s32[]{:S(2)}) async-start(), calls=%async_computation.4 | async-start | bytes 16777216 | tf_op jit(solution)/shard_map/psum | solution.py:99
  353.5 73.8 %copy-start.4 = (bf16[512,4,256]{2,1,0:T(4,128)(2,1)S(1)}, bf16[512,4,256]{2,1,0:T(4,128)(2,1)}, u32[]{:S(2)}) copy-start(bf16[512,4,256]{2,1,0:T(4,128)(2,1)} %reshape.67) | copy-start | bytes 3145732
  436.9 1.6 copy-start.3
  609.7 4.3 copy-start.8
  614.0 2.5 copy-start.7
  616.4 2.6 copy-start.6
  616.4 5.0 copy-start.1
Sparse Core Ops, SparseCore 0:
  437.1 172.5 all-reduce.2
where the time goes:
time: 629 us; the launch traced here: 628 us
  waiting for transfers between devices  488 us (78%)
  matrix products  58.6 us (9%)
  local copies, waits for them, and re-layouts  39 us (6%)
  starting transfers between devices  20.4 us (3%)
  between operations  14.2 us (2%)
  other arithmetic  8.08 us (1%)
    psum x1, waiting for transfers between devices, body(): lax.psum(grad_first.astype(jnp.bfloat16), 'dp').astype(jnp.float32)  161 us
    all_to_all x1, waiting for transfers between devices, body(): lax.all_to_all(first_grad, 'tensor', split_axis=0, concat_axis=0, tiled=T...  87.3 us
    all_to_all x1, waiting for transfers between devices, body(): lax.all_to_all(first_out, 'tensor', split_axis=0, concat_axis=0, tiled=True)  85.9 us
    all_to_all x1, waiting for transfers between devices, body(): lax.all_to_all(third_grad, 'tensor', split_axis=0, concat_axis=0, tiled=T...  82.7 us
    all_to_all x1, waiting for transfers between devices, body(): lax.all_to_all(third_factor_output, 'tensor', split_axis=0, concat_axis=0...  71.2 us
    unnamed x23, local copies, waits for them, and re-layouts  17 us
  transfers between devices with their start and end apart: 5, of which 5 were waited for; matrix products, arithmetic and copies ran while one was open for 9% of the time, Pallas kernels for 0%

commit v1 on v0

--- a/solution.py
+++ b/solution.py
@@ -96,7 +96,7 @@
     )
     grad_first = (grad_first * grad_scale).reshape(width_dev, block_width, hid_blocks * sub_width)
     grad_first, grad_second, grad_third, grad_fourth = (
-        lax.psum(grad_first.astype(jnp.bfloat16), "dp").astype(jnp.float32),
+        jnp.sum(lax.all_gather(grad_first.astype(jnp.bfloat16), "dp"), axis=0).astype(jnp.float32),
         lax.psum(grad_second.astype(jnp.bfloat16), "dp").astype(jnp.float32),
         lax.psum(grad_third.astype(jnp.bfloat16), "dp").astype(jnp.float32),
         lax.psum(grad_fourth.astype(jnp.bfloat16), "dp").astype(jnp.float32),

time: 629 us -> 608 us (0.967); the launches traced: 628 us -> 600 us
  waiting for transfers between devices: 488 us -> 443 us
  other arithmetic: 8.08 us -> 17.2 us
  local copies, waits for them, and re-layouts: 39 us -> 47.9 us
    psum x1, waiting for transfers between devices: 161 us -> 47.5 us  [body(): lax.psum(grad_second.astype(jnp.bfloat16), 'dp').astype(jnp.float32)]
    all_gather x0 -> x1, waiting for transfers between devices: none -> 81 us  [body(): lax.all_gather(grad_first.astype(jnp.bfloat16), 'dp')]
    all_to_all x1, waiting for transfers between devices: 87.3 us -> 68.1 us  [body(): lax.all_to_all(first_grad, 'tensor', split_axis=0, concat_axis=0, tiled=T...]
    reduce_sum x0 -> x1, other arithmetic: none -> 7.53 us  [body(): jnp.sum(lax.all_gather(grad_first.astype(jnp.bfloat16), 'dp'), axis=0)]
    all_to_all x1, waiting for transfers between devices: 71.2 us -> 77.7 us  [body(): lax.all_to_all(third_factor_output, 'tensor', split_axis=0, concat_axis=0...]
    unnamed x23 -> x20, local copies, waits for them, and re-layouts: 17 us -> 20 us
  transfers between devices with their start and end apart: 5 -> 6, of which waited for: 5 -> 6; matrix products, arithmetic and copies ran while one was open for 9% -> 16% of each run, Pallas kernels for 0% -> 0%
where the time goes in v1:
time: 608 us; the launch traced here: 600 us
  waiting for transfers between devices  443 us (73%)
  matrix products  57.2 us (9%)
  local copies, waits for them, and re-layouts  47.9 us (8%)
  starting transfers between devices  20.8 us (3%)
  other arithmetic  17.2 us (3%)
  between operations  14.4 us (2%)
    all_to_all x1, waiting for transfers between devices, body(): lax.all_to_all(first_out, 'tensor', split_axis=0, concat_axis=0, tiled=True)  85.9 us
    all_to_all x1, waiting for transfers between devices, body(): lax.all_to_all(third_grad, 'tensor', split_axis=0, concat_axis=0, tiled=T...  82.8 us
    all_gather x1, waiting for transfers between devices, body(): lax.all_gather(grad_first.astype(jnp.bfloat16), 'dp')  81 us
    all_to_all x1, waiting for transfers between devices, body(): lax.all_to_all(third_factor_output, 'tensor', split_axis=0, concat_axis=0...  77.7 us
    all_to_all x1, waiting for transfers between devices, body(): lax.all_to_all(first_grad, 'tensor', split_axis=0, concat_axis=0, tiled=T...  68.1 us
    psum x1, waiting for transfers between devices, body(): lax.psum(grad_second.astype(jnp.bfloat16), 'dp').astype(jnp.float32)  47.5 us
    unnamed x20, local copies, waits for them, and re-layouts  20 us
  transfers between devices with their start and end apart: 6, of which 6 were waited for; matrix products, arithmetic and copies ran while one was open for 16% of the time, Pallas kernels for 0%

profile of v1, /device:TPU:0, one launch (start us, length us, event | category | flops | bytes accessed | tf_op | source)
XLA Modules:
  0.0 600.3 jit_solution(4896408687683124250)
XLA Ops:
  7.2 0.0 copy-start
  7.2 2.0 reshape.70
  9.2 4.0 copy.63
  13.2 2.9 convert_bitcast_fusion.3
  16.1 2.5 copy.65
  18.5 6.3 %all-to-all-start = ((bf16[8,4,16,8,512]{4,3,2,1,0:T(8,128)(2,1)}), bf16[8,4,16,8,512]{4,3,2,1,0:T(8,128)(2,1)}, u32[]{:S(2)}, u32[]{:S(2)}) async-start(bf16[8,4,16,8,512]{4,3,2,1,0:T(8,128)(2,1)} %copy.65), calls=%async_computation | async-start | bytes 8388608 | tf_op jit(solution)/shard_map/all_to_all | solution.py:37
  24.9 2.6 reshape.77
  27.5 3.1 convert_bitcast_fusion.1
  30.7 2.5 copy.72
  33.1 85.9 %all-to-all-done = bf16[8,4,16,8,512]{4,3,2,1,0:T(8,128)(2,1)} async-done(((bf16[8,4,16,8,512]{4,3,2,1,0:T(8,128)(2,1)}), bf16[8,4,16,8,512]{4,3,2,1,0:T(8,128)(2,1)}, u32[]{:S(2)}, u32[]{:S(2)}) %all-to-all-start) | async-done | bytes 4194336 | tf_op jit(solution)/shard_map/all_to_all | solution.py:37
  119.0 4.6 all-to-all-start.2
  123.6 0.0 copy-done
  123.6 0.0 copy-start.1
  123.6 6.2 %fusion.9 = (bf16[16,256,512]{1,2,0:T(8,128)(2,1)S(1)}, f32[16,512,256,1]{2,1,0,3:T(8,128)}) fusion(bf16[32,16,8,512]{3,2,1,0:T(8,128)(2,1)} %bitcast.3, bf16[16,256,256]{2,1,0:T(8,128)(2,1)S(1)} %copy-done), kind=kOutput, calls=%fused_computation.12 | convolution fusion | flops 1084227584 | bytes 18874368 | tf_op jit(solution)/shard_map/abct,bacj->bjt/dot_general | solution.py:43
  129.8 0.0 copy-start.2
  129.8 0.0 copy-done.1
  129.8 1.3 fusion.57
  131.1 0.7 copy-done.2
  131.8 0.7 convert_bitcast_fusion.2
  132.5 2.4 copy.69
  134.8 82.8 %all-to-all-done.2 = bf16[8,16,4,8,512]{4,3,1,2,0:T(8,128)(2,1)} async-done(((bf16[8,16,4,8,512]{4,3,1,2,0:T(8,128)(2,1)}), bf16[8,16,4,8,512]{4,3,1,2,0:T(8,128)(2,1)}, u32[]{:S(2)}, u32[]{:S(2)}) %all-to-all-start.2) | async-done | bytes 4194336 | tf_op jit(solution)/shard_map/all_to_all | solution.py:70
  217.6 5.1 all-to-all-start.1
  222.6 3.9 copy.67
  226.5 7.9 %fusion.5 = bf16[16,256,512]{1,2,0:T(8,128)(2,1)S(1)} fusion(f32[16,512,256,1]{2,1,0,3:T(8,128)} %get-tuple-element.28, bf16[8,16,4,8,512]{4,3,1,2,0:T(8,128)(2,1)} %all-to-all-done.2, bf16[16,256,8,4,8]{1,4,3,2,0:T(8,128)(2,1)} %bitcast.118), kind=kOutput, calls=%fused_computation.6 | convolution fusion | flops 1094713344 | bytes 18874368 | tf_op jit(solution)/shard_map/gbact,bjgac->bjt/dot_general | solution.py:71
  234.4 0.0 copy-start.4
  234.4 1.3 convert_bitcast_fusion
  235.8 0.7 copy-done.4
  236.4 2.5 copy.76
  238.9 77.7 %all-to-all-done.1 = bf16[8,16,4,8,512]{4,3,2,1,0:T(8,128)(2,1)} async-done(((bf16[8,16,4,8,512]{4,3,2,1,0:T(8,128)(2,1)}), bf16[8,16,4,8,512]{4,3,2,1,0:T(8,128)(2,1)}, u32[]{:S(2)}, u32[]{:S(2)}) %all-to-all-start.1) | async-done | bytes 4194336 | tf_op jit(solution)/shard_map/all_to_all | solution.py:52
  316.6 4.6 all-to-all-start.3
  321.2 0.0 all-reduce.3.cloned.1.call-start
  321.3 6.0 %multiply_convert_fusion.1 = bf16[16,256,8,4,8]{1,4,3,2,0:T(8,128)(2,1)} fusion(bf16[8,16,4,8,512]{4,3,1,2,0:T(8,128)(2,1)} %all-to-all-done.2, bf16[16,256,512]{1,2,0:T(8,128)(2,1)} %copy-done.2), kind=kOutput, calls=%fused_computation.28 | convolution fusion | flops 1075838976 | bytes 10485760 | tf_op jit(solution)/shard_map/bjt,gbact->bjgac/dot_general | solution.py:75
  327.3 4.0 copy.88
  331.3 0.0 copy-start.3
  331.3 6.2 %fusion.33 = bf16[16,256,256]{2,1,0:T(8,128)(2,1)} fusion(bf16[16,256,512]{1,2,0:T(8,128)(2,1)} %copy-done.4, bf16[32,16,8,512]{3,2,1,0:T(8,128)(2,1)} %bitcast.3), kind=kOutput, calls=%fused_computation.36 | convolution fusion | flops 1075838976 | bytes 10485760 | tf_op jit(solution)/shard_map/abct,bjt->bacj/dot_general | solution.py:84
  337.4 0.0 copy-done.3
  337.4 7.0 %multiply_convert_fusion = bf16[4,128,8,256]{3,1,2,0:T(8,128)(2,1)S(1)} fusion(bf16[128,4,8,512]{3,2,1,0:T(8,128)(2,1)} %bitcast.12, bf16[512,4,256,1]{2,1,0,3:T(4,128)(2,1)S(1)} %bitcast.116), kind=kOutput, calls=%fused_computation.27 | convolution fusion | flops 1075838976 | bytes 7340032 | tf_op jit(solution)/shard_map/bact,tak->abck/dot_general | solution.py:66
  344.4 2.5 copy.163
  346.9 0.0 all-reduce.3.cloned.1.call-update
  347.0 0.2 all-gather.2.cloned.1.call-start
  347.2 68.1 %all-to-all-done.3 = bf16[8,16,4,8,512]{4,3,2,1,0:T(8,128)(2,1)} async-done(((bf16[8,16,4,8,512]{4,3,2,1,0:T(8,128)(2,1)}), bf16[8,16,4,8,512]{4,3,2,1,0:T(8,128)(2,1)}, u32[]{:S(2)}, u32[]{:S(2)}) %all-to-all-start.3) | async-done | bytes 4194336 | tf_op jit(solution)/shard_map/all_to_all | solution.py:88
  415.2 7.0 %fusion.32 = bf16[4,256,128,8]{1,2,3,0:T(8,128)(2,1)S(1)} fusion(bf16[128,4,8,512]{3,2,1,0:T(8,128)(2,1)} %bitcast.26, bf16[512,4,256,1]{2,1,0,3:T(4,128)(2,1)S(1)} %bitcast.114), kind=kOutput, calls=%fused_computation.35 | convolution fusion | flops 1075838976 | bytes 7340032 | tf_op jit(solution)/shard_map/tai,bact->aibc/dot_general | solution.py:94
  422.2 2.5 copy.164
  424.7 4.4 copy.82
  429.1 0.0 all-gather.2.cloned.1.call-update
  429.2 4.2 bitcast_convert_fusion
  433.3 1.3 copy.93
  434.7 4.2 bitcast_convert_fusion.1
  438.8 1.3 copy.92
  440.1 47.5 %all-reduce.3.cloned.1.call-done = (bf16[16,256,256]{2,1,0:T(8,128)(2,1)}, bf16[16,256,256]{2,1,0:T(8,128)(2,1)}, bf16[4,1024,256]{2,1,0:T(8,128)(2,1)}) async-done(((bf16[16,256,256]{2,1,0:T(8,128)(2,1)}, bf16[16,256,256]{2,1,0:T(8,128)(2,1)}, bf16[4,1024,256]{2,1,0:T(8,128)(2,1)}), (bf16[16,256,256]{2,1,0:T(8,128)(2,1)}, bf16[16,256,256]{2,1,0:T(8,128)(2,1)}, ...) | async-done | bytes 6291472 | tf_op jit(solution)/shard_map/psum | solution.py:100
  487.6 0.0 copy-start.6
  487.6 4.2 convert_element_type.111
  491.8 0.0 copy-start.5
  491.8 0.0 copy-done.6
  491.8 2.5 convert_element_type.114
  494.3 0.0 copy-done.5
  494.3 2.4 convert_element_type.117
  496.6 81.0 %all-gather.2.cloned.1.call-done = bf16[4,4,256,1024]{3,2,1,0:T(8,128)(2,1)} async-done(((bf16[1,4,256,1024]{3,2,1,0:T(8,128)(2,1)}), bf16[4,4,256,1024]{3,2,1,0:T(8,128)(2,1)}) %all-gather.2.cloned.1.call-update) | async-done | bytes 8388624 | tf_op jit(solution)/shard_map/all_gather | solution.py:99
  577.7 7.5 %reduce_sum.12 = bf16[4,256,1024]{2,1,0:T(8,128)(2,1)} reduce(bf16[4,4,256,1024]{3,2,1,0:T(8,128)(2,1)} %all-gather.2.cloned.1.call-done, bf16[]{:T(256)} %constant.4.clone.1), dimensions={0}, to_apply=%region_0.0 | reduce | flops 3145728 | bytes 10485762 | tf_op jit(solution)/shard_map/reduce_sum | solution.py:99
  585.2 3.9 copy.118
  589.1 4.1 copy.94
Async XLA Ops:
  7.2 116.4 %copy-start = (bf16[16,256,256]{2,1,0:T(8,128)(2,1)S(1)}, bf16[16,256,256]{2,1,0:T(8,128)(2,1)}, u32[]{:S(2)}) copy-start(bf16[16,256,256]{2,1,0:T(8,128)(2,1)} %param.9) | copy-start | bytes 6291460
  18.5 100.4 %all-to-all-start = ((bf16[8,4,16,8,512]{4,3,2,1,0:T(8,128)(2,1)}), bf16[8,4,16,8,512]{4,3,2,1,0:T(8,128)(2,1)}, u32[]{:S(2)}, u32[]{:S(2)}) async-start(bf16[8,4,16,8,512]{4,3,2,1,0:T(8,128)(2,1)} %copy.65), calls=%async_computation | async-start | bytes 8388608 | tf_op jit(solution)/shard_map/all_to_all | solution.py:37
  119.0 98.6 %all-to-all-start.2 = ((bf16[8,16,4,8,512]{4,3,1,2,0:T(8,128)(2,1)}), bf16[8,16,4,8,512]{4,3,1,2,0:T(8,128)(2,1)}, u32[]{:S(2)}, u32[]{:S(2)}) async-start(bf16[8,16,4,8,512]{4,3,1,2,0:T(8,128)(2,1)} %copy.72), calls=%async_computation.2 | async-start | bytes 8388608 | tf_op jit(solution)/shard_map/all_to_all | solution.py:70
  123.6 6.2 %copy-start.1 = (bf16[16,256,256]{2,1,0:T(8,128)(2,1)S(1)}, bf16[16,256,256]{2,1,0:T(8,128)(2,1)}, u32[]{:S(2)}) copy-start(bf16[16,256,256]{2,1,0:T(8,128)(2,1)} %param.10) | copy-start | bytes 6291460
  129.8 2.0 copy-start.2
  217.6 99.1 %all-to-all-start.1 = ((bf16[8,16,4,8,512]{4,3,2,1,0:T(8,128)(2,1)}), bf16[8,16,4,8,512]{4,3,2,1,0:T(8,128)(2,1)}, u32[]{:S(2)}, u32[]{:S(2)}) async-start(bf16[8,16,4,8,512]{4,3,2,1,0:T(8,128)(2,1)} %copy.69), calls=%async_computation.1 | async-start | bytes 8388608 | tf_op jit(solution)/shard_map/all_to_all | solution.py:52
  234.4 2.0 copy-start.4
  316.6 98.6 %all-to-all-start.3 = ((bf16[8,16,4,8,512]{4,3,2,1,0:T(8,128)(2,1)}), bf16[8,16,4,8,512]{4,3,2,1,0:T(8,128)(2,1)}, u32[]{:S(2)}, u32[]{:S(2)}) async-start(bf16[8,16,4,8,512]{4,3,2,1,0:T(8,128)(2,1)} %copy.76), calls=%async_computation.3 | async-start | bytes 8388608 | tf_op jit(solution)/shard_map/all_to_all | solution.py:88
  321.2 166.4 %all-reduce.3.cloned.1.call-start = ((), (), s32[]{:S(2)}) async-start(), calls=%async_computation.5 | async-start | bytes 12582912 | tf_op jit(solution)/shard_map/psum | solution.py:100
  331.3 6.2 %copy-start.3 = (bf16[512,4,256]{2,1,0:T(4,128)(2,1)S(1)}, bf16[512,4,256]{2,1,0:T(4,128)(2,1)}, u32[]{:S(2)}) copy-start(bf16[512,4,256]{2,1,0:T(4,128)(2,1)} %reshape.77) | copy-start | bytes 3145732
  347.0 230.7 %all-gather.2.cloned.1.call-start = ((), (), s32[]{:S(2)}) async-start(), calls=%async_computation.4 | async-start | bytes 10485760 | tf_op jit(solution)/shard_map/all_gather | solution.py:99
  487.6 4.2 copy-start.6
  491.8 2.5 copy-start.5
Sparse Core Ops, SparseCore 0:
  347.1 140.4 all-reduce.2
  490.0 87.5 all-gather.1
